TPU v7x, 32 devices: a whole 2x2x4 slice. The times are simulated.
32 devices in a mesh: dp: 8 (over z, x), seq: 4 (over y, core).
Axes of the slice: x: 2, y: 2, z: 4, core: 2. Of those that a mesh axis runs over, the one named last changes fastest.
Arguments:
- residual_tiles: bfloat16 [8, 1024, 1024], P('dp', 'seq'), may hold values from -16 to 16
- picture_label_tile: int32 [8, 1024], P('dp', 'seq'), may hold values from 0 to 11, never falling along the last dimension, each value on 1 to 512 neighbouring positions
- prenorm_multiplier: float32 [1024], replicated, may hold values from 0.5 to 1.5
- triple_projector: bfloat16 [1024, 3072], P('dp'), may hold values from -0.25 to 0.25
- logit_scaling: float32 [16], replicated, may hold values from 0.3 to 30
- final_projector: bfloat16 [1024, 1024], P('dp'), may hold values from -0.1875 to 0.1875
- binarizer_projector: bfloat16 [1024, 18], replicated, may hold values from -0.1875 to 0.1875
- binarizer_offset: float32 [18], replicated, may hold values from -1 to 1
Outputs:
- mixed: bfloat16 [8, 1024, 1024], P('dp', 'seq')
- bit_codes: float32 [8, 18, 1024], P('dp', None, 'seq')
- code_entropy: float32 [18], replicated
Inputs may be any that keep to these rules, and one draw needn't show every extreme that they name: `picture_label_tile`: in each pack image numbers never fall, every image number of 0 to 11 occurs, and an image has at most 512 patches.
All inputs are finite; a program needn't handle non-finite values.
Results may differ from a plain program's by a relative error of at most 0.0053.
The roundings to bfloat16 on the way count: a program that leaves them out, or rounds other values in their place, can miss the bound.
Values may be sent and summed in bfloat16 or wider, within the bound.
A program may use at most 64 MiB of HBM per device.

v0:
```python
import math

import jax
import jax.numpy as jnp
from jax import lax
from jax.sharding import PartitionSpec as P

epsilon = 1e-06


def rms_scale(values):
    return lax.rsqrt(jnp.mean(values * values, axis=-1, keepdims=True) + epsilon)


def split_subspaces(combined_subspaces, scales, channel_extent):
    token_count = combined_subspaces.shape[0]
    pieces = combined_subspaces.reshape(token_count, 3, scales.shape[0], channel_extent).astype(
        jnp.float32
    )
    asking_tensor = (
        pieces[:, 0] * rms_scale(pieces[:, 0]) * (scales[:, None] / math.sqrt(channel_extent))
    )
    rescaled_lookups = pieces[:, 1] * rms_scale(pieces[:, 1])
    return (
        asking_tensor.astype(jnp.bfloat16),
        rescaled_lookups.astype(jnp.bfloat16),
        pieces[:, 2].astype(jnp.bfloat16),
    )


def on_device(
    residual_tiles,
    picture_label_tile,
    prenorm_multiplier,
    triple_projector,
    logit_scaling,
    final_projector,
    binarizer_projector,
    binarizer_offset,
):
    pack_rows = residual_tiles[0]
    token_rows = pack_rows.shape[0]
    width = pack_rows.shape[1]
    subspace_total = logit_scaling.shape[0]
    channel_extent = width // subspace_total
    wide_pack = pack_rows.astype(jnp.float32)
    normed = (wide_pack * rms_scale(wide_pack) * prenorm_multiplier).astype(jnp.bfloat16)
    query_ids = picture_label_tile[0].astype(jnp.bfloat16)
    gathered, gathered_ids = (
        lax.all_gather(normed, "seq", axis=0, tiled=True),
        lax.all_gather(query_ids, "seq", axis=0, tiled=True),
    )
    seq_length = gathered.shape[0]
    group = lax.axis_size("seq")
    member = lax.axis_index("seq")
    local_heads = subspace_total // group
    shard_rows = triple_projector.shape[0]
    shaped = triple_projector.reshape(shard_rows, 3, subspace_total, channel_extent)
    owned = lax.dynamic_slice_in_dim(shaped, member * local_heads, local_heads, 2).reshape(
        shard_rows, 3 * local_heads * channel_extent
    )
    columns = gathered
    combined_subspaces = jnp.dot(
        columns, lax.all_gather(owned, "dp", axis=0, tiled=True), preferred_element_type=jnp.float32
    ).astype(jnp.bfloat16)
    scales = lax.dynamic_slice_in_dim(logit_scaling, member * local_heads, local_heads, 0)
    asking_tensor, rescaled_lookups, surviving_contents = split_subspaces(
        combined_subspaces, scales, channel_extent
    )
    per_block = 1
    for candidate in range(1, group + 1):
        if group % candidate == 0 and candidate <= max(1, 512 // token_rows):
            per_block = candidate
    block_rows = token_rows * per_block
    query_blocks = asking_tensor.reshape(
        seq_length // block_rows, block_rows, local_heads, channel_extent
    )
    id_blocks = gathered_ids.reshape(seq_length // block_rows, block_rows)

    def attend_block(contraction_operands):
        query_block, id_block = contraction_operands
        same_image = id_block[:, None] == gathered_ids[None, :]
        scores = jnp.einsum(
            "qhd,khd->hqk", query_block, rescaled_lookups, preferred_element_type=jnp.float32
        )
        masked = jnp.where(same_image[None], scores, -1e30)
        highest = jnp.max(masked, axis=-1, keepdims=True)
        probs = jnp.where(same_image[None], jnp.exp(scores - highest), 0.0)
        summed = jnp.einsum(
            "hqk,khd->qhd",
            probs.astype(jnp.bfloat16),
            surviving_contents,
            preferred_element_type=jnp.float32,
        )
        return summed / jnp.swapaxes(jnp.sum(probs, axis=-1), 0, 1)[:, :, None]

    attended = lax.map(attend_block, (query_blocks, id_blocks))
    attended = attended.reshape(seq_length, local_heads * channel_extent).astype(jnp.bfloat16)
    attention = lax.all_to_all(attended, "seq", split_axis=0, concat_axis=1, tiled=True)
    columns = attention
    projected = jnp.dot(
        columns,
        lax.all_gather(final_projector, "dp", axis=0, tiled=True),
        preferred_element_type=jnp.float32,
    )
    mixed = (wide_pack + projected).astype(jnp.bfloat16)
    logits = (
        jnp.dot(mixed, binarizer_projector, preferred_element_type=jnp.float32) + binarizer_offset
    )
    bit_probs = jax.nn.sigmoid(4.0 * logits)
    patch_total = token_rows * lax.axis_size("seq") * lax.axis_size("dp")
    marginal = lax.psum(jnp.sum(bit_probs, axis=0), ("dp", "seq")) / patch_total
    code_entropy = -(marginal * jnp.log(marginal) + (1.0 - marginal) * jnp.log(1.0 - marginal))
    bit_codes = jnp.swapaxes(bit_probs - marginal, 0, 1)[None]
    return (mixed[None], bit_codes, code_entropy)


def solution(mesh):
    return jax.shard_map(
        on_device,
        mesh=mesh,
        in_specs=(
            P("dp", "seq", None),
            P("dp", "seq"),
            P(),
            P("dp", None),
            P(),
            P("dp", None),
            P(),
            P(),
        ),
        out_specs=(P("dp", "seq", None), P("dp", None, "seq"), P()),
        check_vma=False,
    )
```

profile of v0, /device:TPU:0, one launch (start us, length us, event | category | flops | bytes accessed | tf_op | source)
XLA Modules:
  0.0 180.5 jit_solution(10630888551679557100)
XLA Ops:
  7.2 0.0 copy-start
  7.2 0.0 copy-start.10
  7.2 0.0 copy-start.8
  7.2 0.0 all-gather.7.cloned.1.call-start
  7.3 1.5 copy.20
  8.8 0.7 constant_dynamic-slice_fusion
  9.5 0.0 all-gather.7.cloned.1.call-update
  9.5 0.0 all-gather.5.cloned.1.call-start
  9.5 1.2 fusion.44
  10.8 2.1 %fusion.46 = bf16[256,1024]{1,0:T(8,128)(2,1)} fusion(bf16[1,256,1024]{2,1,0:T(8,128)(2,1)} %param.10, f32[1024]{0:T(1024)} %param.12, f32[256]{0:T(256)S(1)} %add_rsqrt_fusion.2), kind=kLoop, calls=%fused_computation.36 | loop fusion | flops 1048576 | bytes 1053696 | tf_op jit(solution)/shard_map/convert_element_type | solution.py:47
  12.8 0.0 all-gather.5.cloned.1.call-update
  12.8 0.0 all-gather.9.cloned.1.call-start
  12.9 0.7 all-gather.9.cloned.1.call-update
  13.6 0.0 copy-done.10
  13.6 0.1 dynamic-slice_multiply_fusion
  13.7 0.0 copy-done.8
  13.7 6.0 %all-gather = bf16[1,1024]{1,0:T(2,128)(2,1)S(1)} all-gather(bf16[1,256]{1,0:T(2,128)(2,1)S(1)} %convert_element_type.50), channel_id=2, replica_groups=mesh['dp'=8,'seq'=4] {'seq'}, dimensions={1}, use_global_device_ids=true | all-gather | bytes 2560 | tf_op jit(solution)/shard_map/all_gather | solution.py:51
  19.8 37.5 %all-gather.7.cloned.1.call-done = bf16[1024,768]{0,1:T(8,128)(2,1)} async-done(((bf16[128,768]{0,1:T(8,128)(2,1)}), bf16[1024,768]{0,1:T(8,128)(2,1)}) %all-gather.7.cloned.1.call-update) | async-done | bytes 1572880 | tf_op jit(solution)/shard_map/all_gather | solution.py:64
  57.2 22.3 %all-gather.5.cloned.1.call-done = bf16[1024,1024]{1,0:T(8,128)(2,1)} async-done(((bf16[256,1024]{1,0:T(8,128)(2,1)}), bf16[1024,1024]{1,0:T(8,128)(2,1)}) %all-gather.5.cloned.1.call-update) | async-done | bytes 2097168 | tf_op jit(solution)/shard_map/all_gather | solution.py:50
  79.6 3.9 %convolution_convert_fusion = bf16[1024,768]{0,1:T(8,128)(2,1)S(1)} fusion(bf16[1024,1024]{1,0:T(8,128)(2,1)} %all-gather.5.cloned.1.call-done, bf16[1024,768]{0,1:T(8,128)(2,1)} %all-gather.7.cloned.1.call-done), kind=kOutput, calls=%fused_computation.23 | convolution fusion | flops 1611399168 | bytes 5242880 | tf_op jit(solution)/shard_map/dot_general | solution.py:63
  83.4 0.0 copy-start.1
  83.4 0.4 convert_element_type.55
  83.8 0.1 multiply_reduce_fusion.1
  84.0 0.1 multiply_reduce_fusion
  84.1 0.5 copy-done.1
  84.6 1.1 slice.15
  85.7 3.1 %squeeze.9 = f32[2,512,4,64]{1,0,3,2:T(2,128)} reshape(f32[1024,1,4,64]{0,3,2,1:T(8,128)} %slice.15) | data formatting | bytes 2097152 | tf_op jit(solution)/shard_map/squeeze | solution.py:21
  88.8 2.0 %slice_bitcast_fusion.1 = bf16[1024,4,64]{0,2,1:T(8,128)(2,1)} fusion(bf16[1024,3,4,64]{0,3,2,1:T(8,128)(2,1)} %bitcast.87), kind=kLoop, calls=%fused_computation.44 | loop fusion | bytes 1048576 | tf_op jit(solution)/shard_map/convert_element_type | solution.py:27
  90.8 0.9 multiply_convert_fusion
  91.7 0.0 copy-done.3
  91.7 0.2 fusion.48
  91.9 23.4 %while.10 = (s32[]{:T(128)}, bf16[2,512,4,64]{1,3,2,0:T(8,128)(2,1)}, bf16[2,512]{1,0:T(2,128)(2,1)S(1)}, bf16[1024]{0:T(1024)(128)(2,1)S(1)}, bf16[2,512,4,64]{...) while((s32[]{:T(128)}, ...), condition=%wide.region_6.7_spmd, body=%wide.region_3.6_spmd.sunk | while | flops 816448512 | bytes 18897072 | solution.py:97
  92.0 0.4 broadcast_compare_fusion.2
  92.3 0.0 copy-start.5
  92.3 0.0 copy-start.6
  92.3 6.9 %fusion.81 = (f32[4,512]{1,0:T(4,128)S(1)}, bf16[4,512,1024]{2,1,0:T(8,128)(2,1)}) fusion(pred[512,1024]{1,0:T(8,128)(4,1)S(1)} %broadcast_compare_fusion.2, bf16[1024,4,64]{0,2,1:T(8,128)(2,1)} %get-tuple-element.140, bf16[2,512,4,64]{1,3,2,0:T(8,128)(2,1)S(1)} %get-tuple-element.139, s32[]{:T(128)} %get-tuple-element.127), kind=kOutput, calls=%fused_computation.56.clone.1 | convolution fusion | flops 547357696 | bytes 6824960 | tf_op jit(solution)/shard_map/while/body/eval_jaxpr/sub | solution.py:88
  99.2 0.0 copy-done.5
  99.2 0.0 copy-done.6
  99.2 3.6 %fusion.82 = bf16[2,512,4,64]{1,3,2,0:T(8,128)(2,1)S(1)} fusion(bf16[2,512,4,64]{1,3,2,0:T(8,128)(2,1)S(1)} %copy-done.6, s32[]{:T(128)} %get-tuple-element.127, bf16[1024,4,64]{0,2,1:T(8,128)(2,1)S(1)} %copy-done.5, bf16[4,512,1024]{2,1,0:T(8,128)(2,1)} %get-tuple-element.117, f32[512,4]{0,1:T(4,128)S(1)} %bitcast.93), kind=kOutput, calls=%fused_computation.11.clone.1 | convolution fusion | flops 268566528 | bytes 5251076 | tf_op jit(solution)/shard_map/while/body/eval_jaxpr/hqk,khd->qhd/dot_general | solution.py:89
  102.8 0.8 copy-done.7
  103.6 0.4 broadcast_compare_fusion.2
  104.0 0.0 copy-start.5
  104.0 0.0 copy-start.6
  104.0 6.9 %fusion.81 = (f32[4,512]{1,0:T(4,128)S(1)}, bf16[4,512,1024]{2,1,0:T(8,128)(2,1)}) fusion(pred[512,1024]{1,0:T(8,128)(4,1)S(1)} %broadcast_compare_fusion.2, bf16[1024,4,64]{0,2,1:T(8,128)(2,1)} %get-tuple-element.140, bf16[2,512,4,64]{1,3,2,0:T(8,128)(2,1)S(1)} %get-tuple-element.139, s32[]{:T(128)} %get-tuple-element.127), kind=kOutput, calls=%fused_computation.56.clone.1 | convolution fusion | flops 547357696 | bytes 6824960 | tf_op jit(solution)/shard_map/while/body/eval_jaxpr/sub | solution.py:88
  110.9 0.0 copy-done.5
  110.9 0.0 copy-done.6
  110.9 3.6 %fusion.82 = bf16[2,512,4,64]{1,3,2,0:T(8,128)(2,1)S(1)} fusion(bf16[2,512,4,64]{1,3,2,0:T(8,128)(2,1)S(1)} %copy-done.6, s32[]{:T(128)} %get-tuple-element.127, bf16[1024,4,64]{0,2,1:T(8,128)(2,1)S(1)} %copy-done.5, bf16[4,512,1024]{2,1,0:T(8,128)(2,1)} %get-tuple-element.117, f32[512,4]{0,1:T(4,128)S(1)} %bitcast.93), kind=kOutput, calls=%fused_computation.11.clone.1 | convolution fusion | flops 268566528 | bytes 5251076 | tf_op jit(solution)/shard_map/while/body/eval_jaxpr/hqk,khd->qhd/dot_general | solution.py:89
  114.5 0.8 copy-done.7
  115.3 1.6 copy.23
  116.9 0.2 convert_element_type.60
  117.1 0.0 copy-start.9
  117.1 0.1 copy.24
  117.2 11.2 %all_to_all.16 = bf16[4,256,256]{1,2,0:T(8,128)(2,1)S(1)} all-to-all(bf16[4,256,256]{1,2,0:T(8,128)(2,1)S(1)} %copy.24), channel_id=1, replica_groups=mesh['dp'=8,'seq'=4] {'seq'}, dimensions={0} | all-to-all | bytes 1048576 | tf_op jit(solution)/shard_map/all_to_all | solution.py:99
  128.4 2.4 %all-gather.9.cloned.1.call-done = bf16[1024,1024]{1,0:T(8,128)(2,1)} async-done(((bf16[128,1024]{1,0:T(8,128)(2,1)}), bf16[1024,1024]{1,0:T(8,128)(2,1)}) %all-gather.9.cloned.1.call-update) | async-done | bytes 2097168 | tf_op jit(solution)/shard_map/all_gather | solution.py:103
  130.8 0.0 copy-done.2
  130.8 2.3 %fusion.38 = bf16[256,1024]{1,0:T(8,128)(2,1)S(1)} fusion(bf16[256,1024]{0,1:T(8,128)(2,1)S(1)} %bitcast.89, bf16[1024,1024]{1,0:T(8,128)(2,1)} %all-gather.9.cloned.1.call-done, bf16[1,256,1024]{2,1,0:T(8,128)(2,1)S(1)} %copy-done.2), kind=kOutput, calls=%fused_computation.27 | convolution fusion | flops 537657344 | bytes 3670016 | tf_op jit(solution)/shard_map/dot_general | solution.py:101
  133.1 0.0 copy-done
  133.2 0.0 copy-start.4
  133.2 0.4 fusion.56
  133.6 39.2 %psum.7 = f32[18]{0:T(128)S(1)} all-reduce(f32[18]{0:T(128)S(1)} %get-tuple-element.68), channel_id=1, replica_groups=mesh['dp'=8,'seq'=4] {'dp','seq'}, use_global_device_ids=true, to_apply=%region_8.9 | all-reduce | flops 18 | bytes 144 | tf_op jit(solution)/shard_map/psum | solution.py:112
  172.8 0.5 fusion.50
  173.3 0.1 subtract_bitcast_fusion
  173.4 0.6 copy.25
  174.0 0.0 copy-done.4
  (14 shorter events, 0.1 us)
Async XLA Ops:
  7.2 126.0 %copy-start = (bf16[1024,18]{0,1:T(8,128)(2,1)S(1)}, bf16[1024,18]{0,1:T(8,128)(2,1)}, u32[]{:S(2)}) copy-start(bf16[1024,18]{0,1:T(8,128)(2,1)} %param.16) | copy-start | bytes 110596
  7.2 6.4 %copy-start.10 = (f32[16]{0:T(128)S(1)}, f32[16]{0:T(128)}, u32[]{:S(2)}) copy-start(f32[16]{0:T(128)} %param.14) | copy-start | bytes 196
  7.2 6.5 %copy-start.8 = (s32[1,256]{1,0:T(1,128)S(1)}, s32[1,256]{1,0:T(1,128)}, u32[]{:S(2)}) copy-start(s32[1,256]{1,0:T(1,128)} %param.11) | copy-start | bytes 3076
  7.2 50.0 %all-gather.7.cloned.1.call-start = ((), (), s32[]{:S(2)}) async-start(), calls=%async_computation.2 | async-start | bytes 1769472 | tf_op jit(solution)/shard_map/all_gather | solution.py:64
  9.5 70.1 %all-gather.5.cloned.1.call-start = ((), (), s32[]{:S(2)}) async-start(), calls=%async_computation.1 | async-start | bytes 2621440 | tf_op jit(solution)/shard_map/all_gather | solution.py:50
  12.8 118.0 %all-gather.9.cloned.1.call-start = ((), (), s32[]{:S(2)}) async-start(), calls=%async_computation.3 | async-start | bytes 2359296 | tf_op jit(solution)/shard_map/all_gather | solution.py:103
  83.4 1.2 copy-start.1
  88.8 2.9 %copy-start.3 = (f32[2,512,4,64]{1,0,3,2:T(2,128)S(1)}, f32[2,512,4,64]{1,0,3,2:T(2,128)}, u32[]{:S(2)}) copy-start(f32[2,512,4,64]{1,0,3,2:T(2,128)} %squeeze.9) | copy-start | bytes 3145732
  92.3 6.9 %copy-start.5 = (bf16[1024,4,64]{0,2,1:T(8,128)(2,1)S(1)}, bf16[1024,4,64]{0,2,1:T(8,128)(2,1)}, u32[]{:S(2)}) copy-start(bf16[1024,4,64]{0,2,1:T(8,128)(2,1)} %get-tuple-element.141) | copy-start | bytes 1572868 | tf_op jit(solution)/shard_map/while
  92.3 6.9 %copy-start.6 = (bf16[2,512,4,64]{1,3,2,0:T(8,128)(2,1)S(1)}, bf16[2,512,4,64]{1,3,2,0:T(8,128)(2,1)}, u32[]{:S(2)}) copy-start(bf16[2,512,4,64]{1,3,2,0:T(8,128)(2,1)} %get-tuple-element.128) | copy-start | bytes 1572868 | tf_op jit(solution)/shard_map/while
  102.8 0.8 copy-start.7
  104.0 6.9 %copy-start.5 = (bf16[1024,4,64]{0,2,1:T(8,128)(2,1)S(1)}, bf16[1024,4,64]{0,2,1:T(8,128)(2,1)}, u32[]{:S(2)}) copy-start(bf16[1024,4,64]{0,2,1:T(8,128)(2,1)} %get-tuple-element.141) | copy-start | bytes 1572868 | tf_op jit(solution)/shard_map/while
  104.0 6.9 %copy-start.6 = (bf16[2,512,4,64]{1,3,2,0:T(8,128)(2,1)S(1)}, bf16[2,512,4,64]{1,3,2,0:T(8,128)(2,1)}, u32[]{:S(2)}) copy-start(bf16[2,512,4,64]{1,3,2,0:T(8,128)(2,1)} %get-tuple-element.128) | copy-start | bytes 1572868 | tf_op jit(solution)/shard_map/while
  114.5 0.8 copy-start.7
  115.3 15.5 %copy-start.2 = (bf16[1,256,1024]{2,1,0:T(8,128)(2,1)S(1)}, bf16[1,256,1024]{2,1,0:T(8,128)(2,1)}, u32[]{:S(2)}) copy-start(bf16[1,256,1024]{2,1,0:T(8,128)(2,1)} %param.10) | copy-start | bytes 1572868
  117.1 16.0 %copy-start.9 = (f32[18]{0:T(128)S(1)}, f32[18]{0:T(128)}, u32[]{:S(2)}) copy-start(f32[18]{0:T(128)} %param.17) | copy-start | bytes 220
  133.2 40.8 %copy-start.4 = (bf16[256,1024]{1,0:T(8,128)(2,1)}, bf16[256,1024]{1,0:T(8,128)(2,1)S(1)}, u32[]{:S(2)}) copy-start(bf16[256,1024]{1,0:T(8,128)(2,1)S(1)} %fusion.38) | copy-start | bytes 1572868
Sparse Core Ops, SparseCore 0:
  10.1 47.1 all-gather.6
  58.8 20.7 all-gather.4
  81.7 49.0 all-gather.8
where the time goes:
time: 181 us
  waiting for transfers between devices  62.9 us (35%)
  blocking collectives  56.5 us (31%)
  matrix products  27.5 us (15%)
  between operations  13.9 us (8%)
  local copies, waits for them, and re-layouts  13.1 us (7%)
  other arithmetic  6.49 us (4%)
    psum x1, blocking collectives, on_device(): marginal = lax.psum(jnp.sum(bit_probs, axis=0), ('dp', 'seq')) / patch_total  39.2 us
    all_gather x1, waiting for transfers between devices, on_device(): lax.all_gather(owned, 'dp', axis=0, tiled=True)  37.5 us
    all_gather x1, waiting for transfers between devices, on_device(): lax.all_gather(normed, 'seq', axis=0, tiled=True)  22.3 us
    sub x2, matrix products, attend_block(): probs = jnp.where(same_image[None], jnp.exp(scores - highest), 0.0)  13.7 us
    all_to_all x1, blocking collectives, on_device(): lax.all_to_all(attended, 'seq', split_axis=0, concat_axis=1, tiled=True)  11.2 us
    dot_general x2, matrix products, attend_block(): jnp.einsum('hqk,khd->qhd', probs.astype(jnp.bfloat16), surviving_contents...  7.18 us
    all_gather x1, blocking collectives, on_device(): lax.all_gather(query_ids, 'seq', axis=0, tiled=True)  6.03 us
    dot_general x1, matrix products, on_device(): jnp.dot(columns, lax.all_gather(owned, 'dp', axis=0, tiled=True), preferr...  3.86 us
  transfers between devices with their start and end apart: 3, of which 3 were waited for; matrix products, arithmetic and copies ran while one was open for 22% of the time, Pallas kernels for 0%

commit v1 on v0

v1 whole, which is shorter than its diff:
```python
import functools
import math

import jax
import jax.numpy as jnp
from jax import lax
from jax.experimental import pallas as pl
from jax.experimental.pallas import tpu as pltpu
from jax.sharding import PartitionSpec as P

EPS = 1e-06
MESH = pl.DeviceIdType.MESH
NEG = -1e30


def layer_kernel(
    cfg,
    x_ref,
    ids_ref,
    gain_ref,
    w_ref,
    scale_ref,
    wo_ref,
    bits_ref,
    off_ref,
    mixed_ref,
    codes_ref,
    ent_ref,
    wg,
    wog,
    xg,
    idg,
    idcol,
    normed,
    acc,
    qs,
    ks,
    vs,
    ao,
    ag,
    part1,
    part2,
    local_sem,
    wz_s,
    wz_r,
    wx_s,
    wx_r,
    oz_s,
    oz_r,
    ox_s,
    ox_r,
    oy_s,
    oy_r,
    oc_s,
    oc_r,
    xy_s,
    xy_r,
    xc_s,
    xc_r,
    id_s,
    id_r,
    at_s,
    at_r,
    p1_s,
    p1_r,
    p2_s,
    p2_r,
):
    nz, nx, ny, nc = cfg["nz"], cfg["nx"], cfg["ny"], cfg["nc"]
    n = ny * nc
    ndp = nz * nx
    heads, channel = cfg["heads"], cfg["channel"]
    rows, width = x_ref.shape
    shard = w_ref.shape[0]
    chunk = nx * shard
    cols = width // n
    seq_len = rows * n
    bits = bits_ref.shape[0]
    dp = lax.axis_index("dp")
    me = lax.axis_index("seq")
    z = dp // nx
    x = dp % nx
    y = me // nc
    core = me % nc

    def dp_at(zz, xx):
        return zz * nx + xx

    def seq_at(yy, cc):
        return yy * nc + cc

    def remote(src, dst, ss, rs, d, s):
        return pltpu.make_async_remote_copy(
            src_ref=src, dst_ref=dst, send_sem=ss, recv_sem=rs, device_id=(d, s), device_id_type=MESH
        )

    def w_slot(zz, xx):
        return wg.at[zz, pl.ds(pl.multiple_of(xx * shard, shard), shard), :]

    def o_slot(zz, xx):
        return wog.at[me, pl.ds(pl.multiple_of(dp_at(zz, xx) * shard, shard), shard), :]

    own = []
    for part in range(3):
        own.append(
            pltpu.make_async_copy(
                w_ref.at[:, pl.ds(pl.multiple_of(part * width + me * cols, 128), cols)],
                wg.at[
                    z,
                    pl.ds(pl.multiple_of(x * shard, shard), shard),
                    pl.ds(part * cols, cols),
                ],
                local_sem.at[part],
            )
        )
    own.append(pltpu.make_async_copy(x_ref, xg.at[me], local_sem.at[3]))
    own.append(pltpu.make_async_copy(ids_ref, idg.at[me], local_sem.at[4]))
    own.append(
        pltpu.make_async_copy(
            wo_ref.at[:, pl.ds(pl.multiple_of(me * cols, 128), cols)], o_slot(z, x), local_sem.at[5]
        )
    )
    for c in own:
        c.start()

    barrier = pltpu.get_barrier_semaphore()

    def greet_seq(i, _):
        pl.semaphore_signal(
            barrier, inc=1, device_id=(dp, (me + i) % n), device_id_type=MESH
        )
        return 0

    def greet_dp(i, _):
        pl.semaphore_signal(
            barrier, inc=1, device_id=((dp + i) % ndp, me), device_id_type=MESH
        )
        return 0

    lax.fori_loop(1, n, greet_seq, 0)
    lax.fori_loop(1, ndp, greet_dp, 0)
    pl.semaphore_wait(barrier, n - 1 + ndp - 1)

    sends = []

    def go(c):
        c.start()
        sends.append(c)

    own[0].wait()
    own[1].wait()
    own[2].wait()
    for i in range(1, nz):
        go(remote(w_slot(z, x), w_slot(z, x), wz_s.at[i], wz_r.at[i], dp_at((z + i) % nz, x), me))
    for k in range(1, nx):
        go(remote(w_slot(z, x), w_slot(z, x), wx_s.at[0, k], wx_r.at[0, k], dp_at(z, (x + k) % nx), me))
    own[3].wait()
    for i in range(1, ny):
        go(remote(xg.at[me], xg.at[me], xy_s.at[i], xy_r.at[i], dp, seq_at((y + i) % ny, core)))
    for k in range(1, nc):
        go(remote(xg.at[me], xg.at[me], xc_s.at[0, k], xc_r.at[0, k], dp, seq_at(y, (core + k) % nc)))
    own[4].wait()
    for i in range(1, n):
        go(remote(idg.at[me], idg.at[me], id_s.at[i], id_r.at[i], dp, (me + i) % n))
    own[5].wait()
    for i in range(1, nz):
        go(remote(o_slot(z, x), o_slot(z, x), oz_s.at[i], oz_r.at[i], dp_at((z + i) % nz, x), me))
    for k in range(1, nx):
        go(remote(o_slot(z, x), o_slot(z, x), ox_s.at[0, k], ox_r.at[0, k], dp_at(z, (x + k) % nx), me))

    gain = gain_ref[...]

    def norm_rows(member):
        base = pl.multiple_of(member * rows, rows)

        def body(b, _):
            r0 = pl.multiple_of(b * 64, 64)
            wide = xg[member, pl.ds(r0, 64), :].astype(jnp.float32)
            ms = jnp.mean(wide * wide, axis=-1, keepdims=True)
            out = (wide * lax.rsqrt(ms + EPS) * gain).astype(jnp.bfloat16)
            for g in range(nz):
                normed[g, pl.ds(base + r0, 64), :] = out[:, g * chunk : (g + 1) * chunk]
            return 0

        lax.fori_loop(0, rows // 64, body, 0)

    def arrive(slot, sem):
        remote(slot, slot, sem, sem, dp, me).wait_recv()

    def w_forward(i):
        zz = (z - i + nz) % nz
        arrive(w_slot(zz, x), wz_r.at[i])
        for k in range(1, nx):
            go(remote(w_slot(zz, x), w_slot(zz, x), wx_s.at[i, k], wx_r.at[i, k], dp_at(z, (x + k) % nx), me))

    norm_rows(me)
    for k in range(1, nc):
        other = seq_at(y, (core - k + nc) % nc)
        arrive(xg.at[other], xc_r.at[0, k])
        norm_rows(other)
    for i in range(1, nz - 1):
        w_forward(i)
    for i in range(1, ny):
        yy = (y - i + ny) % ny
        source = seq_at(yy, core)
        arrive(xg.at[source], xy_r.at[i])
        for k in range(1, nc):
            go(remote(xg.at[source], xg.at[source], xc_s.at[i, k], xc_r.at[i, k], dp, seq_at(y, (core + k) % nc)))
        norm_rows(source)
    for i in range(1, ny):
        yy = (y - i + ny) % ny
        for k in range(1, nc):
            other = seq_at(yy, (core - k + nc) % nc)
            arrive(xg.at[other], xc_r.at[i, k])
            norm_rows(other)

    for i in range(1, n):
        arrive(idg.at[(me - i + n) % n], id_r.at[i])
    for m in range(n):
        line = jnp.broadcast_to(idg[m].astype(jnp.float32), (128, rows))
        idcol[pl.ds(m * rows, rows), :] = jnp.transpose(line)
    id_row = jnp.concatenate([idg[m] for m in range(n)], axis=1).astype(jnp.float32)

    row_block = 256
    blocks = seq_len // row_block

    def project(i, first):
        zz = (z - i + nz) % nz
        for k in range(1, nx):
            arrive(w_slot(zz, (x - k + nx) % nx), wx_r.at[i, k])

        def body(b, _):
            r = pl.ds(pl.multiple_of(b * row_block, row_block), row_block)
            prod = jnp.dot(normed[zz, r, :], wg[zz], preferred_element_type=jnp.float32)
            if first:
                acc[r, :] = prod
            else:
                acc[r, :] = acc[r, :] + prod
            return 0

        lax.fori_loop(0, blocks, body, 0)

    for i in range(nz):
        if i == max(0, nz - 2):
            if nz > 1:
                w_forward(nz - 1)
        project(i, i == 0)

    def group_of(shape, dim):
        return lax.div(lax.broadcasted_iota(jnp.int32, shape, dim), jnp.int32(channel))

    same_head = (group_of((cols, cols), 0) == group_of((cols, cols), 1)).astype(jnp.float32)
    same_head = same_head.astype(jnp.bfloat16)
    scale_row = scale_ref[:, pl.ds(pl.multiple_of(me * cols, 128), cols)] / math.sqrt(channel)

    def head_scale(values):
        square = values * values
        high = square.astype(jnp.bfloat16)
        low = (square - high.astype(jnp.float32)).astype(jnp.bfloat16)
        total = jnp.dot(high, same_head, preferred_element_type=jnp.float32) + jnp.dot(
            low, same_head, preferred_element_type=jnp.float32
        )
        return lax.rsqrt(total / channel + EPS)

    def split(b, _):
        r = pl.ds(pl.multiple_of(b * row_block, row_block), row_block)
        joined = acc[r, :].astype(jnp.bfloat16)
        q = joined[:, :cols].astype(jnp.float32)
        k = joined[:, cols : 2 * cols].astype(jnp.float32)
        qs[r, :] = (q * head_scale(q) * scale_row).astype(jnp.bfloat16)
        ks[r, :] = (k * head_scale(k)).astype(jnp.bfloat16)
        vs[r, :] = joined[:, 2 * cols :]
        return 0

    lax.fori_loop(0, blocks, split, 0)

    for i in range(1, nz):
        zz = (z - i + nz) % nz
        arrive(o_slot(zz, x), oz_r.at[i])
        for k in range(1, nx):
            go(remote(o_slot(zz, x), o_slot(zz, x), ox_s.at[i, k], ox_r.at[i, k], dp_at(z, (x + k) % nx), me))

    q_block = cfg["q_block"]
    lane_head = group_of((q_block, cols), 1)

    def stage_target(t, sign):
        dy = (t // nc + 1) % ny
        dc = (t + 1) % nc
        if sign > 0:
            return seq_at((y + dy) % ny, (core + dc) % nc)
        return seq_at((y - dy + ny) % ny, (core - dc + nc) % nc)

    def a2a(t):
        j = stage_target(t, 1)
        return remote(ao.at[j], ag.at[me], at_s.at[t], at_r.at[t], dp, j)

    oy = [
        remote(wog.at[me], wog.at[me], oy_s.at[i], oy_r.at[i], dp, seq_at((y + i) % ny, core))
        for i in range(1, ny)
    ]
    oc = [
        remote(wog.at[me], wog.at[me], oc_s.at[0, k], oc_r.at[0, k], dp, seq_at(y, (core + k) % nc))
        for k in range(1, nc)
    ]
    oc_late = []
    for i in range(1, ny):
        source = seq_at((y - i + ny) % ny, core)
        for k in range(1, nc):
            oc_late.append(
                remote(wog.at[source], wog.at[source], oc_s.at[i, k], oc_r.at[i, k], dp, seq_at(y, (core + k) % nc))
            )

    def stage(t, _):
        j = stage_target(t, 1)
        for sub in range(rows // q_block):
            r = pl.ds(pl.multiple_of(j * rows + sub * q_block, q_block), q_block)
            bias = jnp.where(idcol[r, :][:, :1] == id_row, 0.0, NEG)
            qb = qs[r, :]
            out = jnp.zeros((q_block, cols), jnp.float32)
            for h in range(heads):
                mine = lane_head == h
                qh = jnp.where(mine, qb, jnp.zeros_like(qb))
                s = lax.dot_general(
                    qh, ks[...], (((1,), (1,)), ((), ())), preferred_element_type=jnp.float32
                )
                s = s + bias
                p = jnp.exp(s - jnp.max(s, axis=-1, keepdims=True))
                total = jnp.sum(p, axis=-1, keepdims=True)
                o = jnp.dot(p.astype(jnp.bfloat16), vs[...], preferred_element_type=jnp.float32)
                out = jnp.where(mine, o / total, out)
            ao[j, pl.ds(sub * q_block, q_block), :] = out.astype(jnp.bfloat16)

        @pl.when(t < n - 1)
        def _():
            a2a(t).start()

        @pl.when(t == 0)
        def _():
            for i in range(nz):
                zz = (z - i + nz) % nz
                for k in range(1, nx):
                    arrive(o_slot(zz, (x - k + nx) % nx), ox_r.at[i, k])
            for c in oy + oc:
                c.start()

        @pl.when(t == n - 2)
        def _():
            for i in range(1, ny):
                arrive(wog.at[seq_at((y - i + ny) % ny, core)], oy_r.at[i])
            for c in oc_late:
                c.start()

        return 0

    lax.fori_loop(0, n, stage, 0)
    sends.extend(oy + oc + oc_late)

    for i in range(ny):
        for k in range(1, nc):
            arrive(wog.at[seq_at((y - i + ny) % ny, (core - k + nc) % nc)], oc_r.at[i, k])
    for t in range(n - 1):
        arrive(ag.at[stage_target(t, -1)], at_r.at[t])
    ag[me] = ao[me]

    attention = jnp.concatenate([ag[m] for m in range(n)], axis=1)
    for g in range(n):
        lanes = slice(g * cols, (g + 1) * cols)
        prod = jnp.dot(attention, wog[g], preferred_element_type=jnp.float32)
        mixed_ref[:, lanes] = (xg[me, :, lanes].astype(jnp.float32) + prod).astype(jnp.bfloat16)

    logits = lax.dot_general(
        bits_ref[...], mixed_ref[...], (((1,), (1,)), ((), ())), preferred_element_type=jnp.float32
    )
    probs = jax.nn.sigmoid(4.0 * (logits + off_ref[...]))
    part1[me, :, :] = jnp.broadcast_to(jnp.sum(probs, axis=1, keepdims=True), (bits, 128))
    for i in range(1, n):
        go(remote(part1.at[me], part1.at[me], p1_s.at[i], p1_r.at[i], dp, (me + i) % n))
    for i in range(1, n):
        arrive(part1.at[(me - i + n) % n], p1_r.at[i])
    pack = part1[0]
    for m in range(1, n):
        pack = pack + part1[m]
    part2[dp, :, :] = pack
    for i in range(1, ndp):
        go(remote(part2.at[dp], part2.at[dp], p2_s.at[i], p2_r.at[i], (dp + i) % ndp, me))
    for i in range(1, ndp):
        arrive(part2.at[(dp - i + ndp) % ndp], p2_r.at[i])
    total = part2[0]
    for m in range(1, ndp):
        total = total + part2[m]
    marginal = total / (seq_len * ndp)
    ent_ref[...] = -(marginal * jnp.log(marginal) + (1.0 - marginal) * jnp.log(1.0 - marginal))
    codes_ref[...] = probs - marginal[:, :1]

    for c in sends:
        c.wait_send()
    for t in range(n - 1):
        a2a(t).wait_send()


def on_device(
    cfg,
    residual_tiles,
    picture_label_tile,
    prenorm_multiplier,
    triple_projector,
    logit_scaling,
    final_projector,
    binarizer_projector,
    binarizer_offset,
):
    nz, nx, ny, nc = cfg["nz"], cfg["nx"], cfg["ny"], cfg["nc"]
    n, ndp = ny * nc, nz * nx
    _, rows, width = residual_tiles.shape
    heads_all = logit_scaling.shape[0]
    bits = binarizer_projector.shape[1]
    cols = width // n
    shard = triple_projector.shape[0]
    seq_len = rows * n
    cfg = dict(cfg, heads=heads_all // n, channel=width // heads_all, q_block=min(256, rows))
    dma = pltpu.SemaphoreType.DMA
    vmem, hbm = pl.BlockSpec(memory_space=pltpu.VMEM), pl.BlockSpec(memory_space=pl.ANY)
    bf16, f32 = jnp.bfloat16, jnp.float32
    mixed, codes, ent = pl.pallas_call(
        functools.partial(layer_kernel, cfg),
        out_shape=(
            jax.ShapeDtypeStruct((rows, width), bf16),
            jax.ShapeDtypeStruct((bits, rows), f32),
            jax.ShapeDtypeStruct((bits, 128), f32),
        ),
        in_specs=[hbm, vmem, vmem, hbm, vmem, hbm, vmem, vmem],
        out_specs=(vmem, vmem, vmem),
        scratch_shapes=[
            pltpu.VMEM((nz, nx * shard, 3 * cols), bf16),
            pltpu.VMEM((n, width, cols), bf16),
            pltpu.VMEM((n, rows, width), bf16),
            pltpu.VMEM((n, 1, rows), jnp.int32),
            pltpu.VMEM((seq_len, 128), f32),
            pltpu.VMEM((nz, seq_len, nx * shard), bf16),
            pltpu.VMEM((seq_len, 3 * cols), f32),
            pltpu.VMEM((seq_len, cols), bf16),
            pltpu.VMEM((seq_len, cols), bf16),
            pltpu.VMEM((seq_len, cols), bf16),
            pltpu.VMEM((n, rows, cols), bf16),
            pltpu.VMEM((n, rows, cols), bf16),
            pltpu.VMEM((n, bits, 128), f32),
            pltpu.VMEM((ndp, bits, 128), f32),
            dma((6,)),
            dma((nz,)),
            dma((nz,)),
            dma((nz, nx)),
            dma((nz, nx)),
            dma((nz,)),
            dma((nz,)),
            dma((nz, nx)),
            dma((nz, nx)),
            dma((ny,)),
            dma((ny,)),
            dma((ny, nc)),
            dma((ny, nc)),
            dma((ny,)),
            dma((ny,)),
            dma((ny, nc)),
            dma((ny, nc)),
            dma((n,)),
            dma((n,)),
            dma((n,)),
            dma((n,)),
            dma((n,)),
            dma((n,)),
            dma((ndp,)),
            dma((ndp,)),
        ],
        compiler_params=pltpu.CompilerParams(
            collective_id=0, has_side_effects=True, vmem_limit_bytes=60 * 1024 * 1024
        ),
        name="layer",
    )(
        residual_tiles[0],
        picture_label_tile,
        prenorm_multiplier[None],
        triple_projector,
        jnp.repeat(logit_scaling, width // heads_all)[None],
        final_projector,
        binarizer_projector.T,
        binarizer_offset[:, None],
    )
    return mixed[None], codes[None], ent[:, 0]


def solution(mesh):
    ndp, n = mesh.shape["dp"], mesh.shape["seq"]
    nx = math.isqrt(ndp // 2)
    if nx < 1 or ndp % nx:
        nx = 1
    nc = 2 if n % 2 == 0 else 1
    cfg = {"nz": ndp // nx, "nx": nx, "ny": n // nc, "nc": nc}
    return jax.shard_map(
        functools.partial(on_device, cfg),
        mesh=mesh,
        in_specs=(
            P("dp", "seq", None),
            P("dp", "seq"),
            P(),
            P("dp", None),
            P(),
            P("dp", None),
            P(),
            P(),
        ),
        out_specs=(P("dp", "seq", None), P("dp", None, "seq"), P()),
        check_vma=False,
    )
```

time: 181 us -> 79.6 us (0.44)
  Pallas kernels: 0 us -> 72.7 us
  waiting for transfers between devices: 62.9 us -> 0 us
  blocking collectives: 56.5 us -> 0 us
  matrix products: 27.5 us -> 0 us
  between operations: 13.9 us -> 0.66 us
  local copies, waits for them, and re-layouts: 13.1 us -> 5.95 us
  other arithmetic: 6.49 us -> 0 us
    pallas_call x0 -> x1, Pallas kernels: none -> 72.7 us  [on_device(): pl.pallas_call(functools.partial(layer_kernel, cfg), out_shape=(jax.Shape...]
    all_gather x3 -> x0, waiting for transfers between devices: 62.2 us -> none  [the longest x1 37.5 us: on_device(): lax.all_gather(owned, 'dp', axis=0, tiled=True)]
    psum x1 -> x0, blocking collectives: 39.2 us -> none  [on_device(): marginal = lax.psum(jnp.sum(bit_probs, axis=0), ('dp', 'seq')) / patch_total]
    dot_general x5 -> x0, matrix products: 13.7 us -> none  [the longest x2 7.18 us: attend_block(): jnp.einsum('hqk,khd->qhd', probs.astype(jnp.bfloat16), surviving_contents...]
    sub x2 -> x0, matrix products: 13.7 us -> none  [attend_block(): probs = jnp.where(same_image[None], jnp.exp(scores - highest), 0.0)]
    all_to_all x1 -> x0, blocking collectives: 11.2 us -> none  [on_device(): lax.all_to_all(attended, 'seq', split_axis=0, concat_axis=1, tiled=True)]
    all_gather x1 -> x0, blocking collectives: 6.03 us -> none  [on_device(): lax.all_gather(query_ids, 'seq', axis=0, tiled=True)]
    convert_element_type x4 -> x0, local copies, waits for them, and re-layouts: 3.9 us -> none  [the longest x1 1.99 us: split_subspaces(): pieces[:, 2].astype(jnp.bfloat16)]
  transfers between devices with their start and end apart: 3 -> 0, of which waited for: 3 -> 0; matrix products, arithmetic and copies ran while one was open for 22% -> 0% of each run, Pallas kernels for 0% -> 0%
where the time goes in v1:
time: 79.6 us; the launch traced here: 79.3 us
  Pallas kernels  72.7 us (91%)
  local copies, waits for them, and re-layouts  5.95 us (7%)
    pallas_call x1, Pallas kernels, on_device(): pl.pallas_call(functools.partial(layer_kernel, cfg), out_shape=(jax.Shape...  72.7 us
    unnamed x8, local copies, waits for them, and re-layouts  3.89 us

profile of v1, /device:TPU:0, one launch (start us, length us, event | category | flops | bytes accessed | tf_op | source)
XLA Modules:
  0.0 79.3 jit_solution(3906643572067176142)
XLA Ops:
  0.6 0.0 copy-start.1
  0.6 0.6 copy-done.1
  1.3 0.1 broadcast_in_dim.16
  1.4 0.0 copy-start.2
  1.4 0.7 broadcast_in_dim_reshape.3.scale_ref
  2.0 0.0 copy-done.2
  2.0 0.7 copy.13.off_ref
  2.7 72.7 %layer.1 = (bf16[256,1024]{1,0:T(8,128)(2,1)}, f32[18,256]{1,0:T(8,128)}, f32[18,128]{1,0:T(8,128)}) custom-call(bf16[256,1024]{1,0:T(8,128)(2,1)} %bitcast.7, s32[1,256]{1,0:T(1,128)} %ids_ref.1, f32[1,1024]{1,0:T(1,128)} %bitcast.10, bf16[128,3072]{1,0:T(8,128)(2,1)} %w_ref.1, f32[1,1024]{1,0:T(1,128)} %broadcast_in_dim_reshape.3.scale_ref, ...), custom_call_target="tpu_custom_call" | custom-call | tf_op jit(solution)/shard_map/layer/pallas_call | solution.py:424
  75.4 0.0 copy-start
  75.4 1.4 %copy.14 = f32[1,18,256]{2,0,1:T(1,128)} copy(f32[1,18,256]{2,1,0:T(8,128)} %bitcast.9) | data formatting | bytes 36864
  76.8 0.0 copy-done
  76.8 0.6 slice_reduce_fusion
  77.4 1.9 %copy.16 = bf16[1,256,1024]{2,1,0:T(8,128)(2,1)} copy(bf16[1,256,1024]{2,1,0:T(8,128)(2,1)} %bitcast.6) | data formatting | bytes 1048576
Async XLA Ops:
  0.6 0.7 copy-start.1
  1.4 0.7 copy-start.2
  75.4 1.4 %copy-start = (f32[18,128]{1,0:T(8,128)S(1)}, f32[18,128]{1,0:T(8,128)}, u32[]{:S(2)}) copy-start(f32[18,128]{1,0:T(8,128)} %get-tuple-element.8) | copy-start | bytes 27652

commit v2 on v1

--- a/solution.py
+++ b/solution.py
@@ -49,8 +49,6 @@
     oz_r,
     ox_s,
     ox_r,
-    oy_s,
-    oy_r,
     oc_s,
     oc_r,
     xy_s,
@@ -78,6 +76,7 @@
     bits = bits_ref.shape[0]
     dp = lax.axis_index("dp")
     me = lax.axis_index("seq")
+    late = cfg["late"]
     z = dp // nx
     x = dp % nx
     y = me // nc
@@ -94,11 +93,96 @@
             src_ref=src, dst_ref=dst, send_sem=ss, recv_sem=rs, device_id=(d, s), device_id_type=MESH
         )
 
+    sends = []
+
+    def go(c):
+        c.start()
+        sends.append(c)
+
+    def arrive(slot, sem):
+        remote(slot, slot, sem, sem, dp, me).wait_recv()
+
     def w_slot(zz, xx):
         return wg.at[zz, pl.ds(pl.multiple_of(xx * shard, shard), shard), :]
 
     def o_slot(zz, xx):
-        return wog.at[me, pl.ds(pl.multiple_of(dp_at(zz, xx) * shard, shard), shard), :]
+        return wog.at[core, pl.ds(pl.multiple_of(dp_at(zz, xx) * shard, shard), shard), :]
+
+    lo = jnp.minimum(z, nz - 1 - z)
+
+    def piece(i):
+        near = z - (i + 1) // 2 if i % 2 else z + (i + 1) // 2
+        far = jnp.where(z > nz - 1 - z, z - (i - lo), z + (i - lo))
+        return jnp.where(i <= 2 * lo, near, far) if i else z
+
+    def first_hops(slot, ss, rs):
+        left = remote(slot(z, x), slot(z, x), ss.at[nz], rs.at[z], dp_at(jnp.maximum(z - 1, 0), x), me)
+        right = remote(
+            slot(z, x), slot(z, x), ss.at[nz + 1], rs.at[z], dp_at(jnp.minimum(z + 1, nz - 1), x), me
+        )
+        return left, right
+
+    def next_hops(slot, ss, rs, i):
+        p = piece(i)
+        left = remote(slot(p, x), slot(p, x), ss.at[p], rs.at[p], dp_at(jnp.maximum(z - 1, 0), x), me)
+        right = remote(
+            slot(p, x), slot(p, x), ss.at[p], rs.at[p], dp_at(jnp.minimum(z + 1, nz - 1), x), me
+        )
+        return left, right
+
+    line_sends = []
+
+    def line_start(slot, ss, rs, i):
+        if nz == 1:
+            return
+        p = piece(i)
+        left, right = next_hops(slot, ss, rs, i) if i else first_hops(slot, ss, rs)
+        to_left = jnp.logical_and(p >= z, z > 0)
+        to_right = jnp.logical_and(p <= z, z < nz - 1)
+        line_sends.append((to_left, left))
+        line_sends.append((to_right, right))
+
+        @pl.when(to_left)
+        def _():
+            left.start()
+
+        @pl.when(to_right)
+        def _():
+            right.start()
+
+    def across(slot, ss, rs, i):
+        p = piece(i)
+        for k in range(1, nx):
+            go(remote(slot(p, x), slot(p, x), ss.at[p, k], rs.at[p, k], dp_at(z, (x + k) % nx), me))
+
+    def shared(p, xx, k):
+        idx = dp_at(p, xx)
+        slot = o_slot(p, xx)
+        return remote(slot, slot, oc_s.at[idx, k], oc_r.at[idx, k], dp, seq_at(y, (core + k) % nc))
+
+    def share(p, xx):
+        for k in range(1, nc):
+            shared(p, xx, k).start()
+
+    def w_relay(i):
+        p = piece(i)
+        arrive(w_slot(p, x), wz_r.at[p])
+        line_start(w_slot, wz_s, wz_r, i)
+        across(w_slot, wx_s, wx_r, i)
+
+    def o_relay(i):
+        p = piece(i)
+        arrive(o_slot(p, x), oz_r.at[p])
+        line_start(o_slot, oz_s, oz_r, i)
+        across(o_slot, ox_s, ox_r, i)
+        share(p, x)
+
+    def o_crossed(i):
+        p = piece(i)
+        for k in range(1, nx):
+            xx = (x - k + nx) % nx
+            arrive(o_slot(p, xx), ox_r.at[p, k])
+            share(p, xx)
 
     own = []
     for part in range(3):
@@ -117,7 +201,9 @@
     own.append(pltpu.make_async_copy(ids_ref, idg.at[me], local_sem.at[4]))
     own.append(
         pltpu.make_async_copy(
-            wo_ref.at[:, pl.ds(pl.multiple_of(me * cols, 128), cols)], o_slot(z, x), local_sem.at[5]
+            wo_ref.at[:, pl.ds(pl.multiple_of(core * (width // nc), 128), width // nc)],
+            o_slot(z, x),
+            local_sem.at[5],
         )
     )
     for c in own:
@@ -141,19 +227,11 @@
     lax.fori_loop(1, ndp, greet_dp, 0)
     pl.semaphore_wait(barrier, n - 1 + ndp - 1)
 
-    sends = []
-
-    def go(c):
-        c.start()
-        sends.append(c)
-
     own[0].wait()
     own[1].wait()
     own[2].wait()
-    for i in range(1, nz):
-        go(remote(w_slot(z, x), w_slot(z, x), wz_s.at[i], wz_r.at[i], dp_at((z + i) % nz, x), me))
-    for k in range(1, nx):
-        go(remote(w_slot(z, x), w_slot(z, x), wx_s.at[0, k], wx_r.at[0, k], dp_at(z, (x + k) % nx), me))
+    line_start(w_slot, wz_s, wz_r, 0)
+    across(w_slot, wx_s, wx_r, 0)
     own[3].wait()
     for i in range(1, ny):
         go(remote(xg.at[me], xg.at[me], xy_s.at[i], xy_r.at[i], dp, seq_at((y + i) % ny, core)))
@@ -163,10 +241,10 @@
     for i in range(1, n):
         go(remote(idg.at[me], idg.at[me], id_s.at[i], id_r.at[i], dp, (me + i) % n))
     own[5].wait()
-    for i in range(1, nz):
-        go(remote(o_slot(z, x), o_slot(z, x), oz_s.at[i], oz_r.at[i], dp_at((z + i) % nz, x), me))
-    for k in range(1, nx):
-        go(remote(o_slot(z, x), o_slot(z, x), ox_s.at[0, k], ox_r.at[0, k], dp_at(z, (x + k) % nx), me))
+    if not late:
+        line_start(o_slot, oz_s, oz_r, 0)
+        across(o_slot, ox_s, ox_r, 0)
+    share(z, x)
 
     gain = gain_ref[...]
 
@@ -184,22 +262,13 @@
 
         lax.fori_loop(0, rows // 64, body, 0)
 
-    def arrive(slot, sem):
-        remote(slot, slot, sem, sem, dp, me).wait_recv()
-
-    def w_forward(i):
-        zz = (z - i + nz) % nz
-        arrive(w_slot(zz, x), wz_r.at[i])
-        for k in range(1, nx):
-            go(remote(w_slot(zz, x), w_slot(zz, x), wx_s.at[i, k], wx_r.at[i, k], dp_at(z, (x + k) % nx), me))
-
     norm_rows(me)
     for k in range(1, nc):
         other = seq_at(y, (core - k + nc) % nc)
         arrive(xg.at[other], xc_r.at[0, k])
         norm_rows(other)
     for i in range(1, nz - 1):
-        w_forward(i)
+        w_relay(i)
     for i in range(1, ny):
         yy = (y - i + ny) % ny
         source = seq_at(yy, core)
@@ -225,9 +294,9 @@
     blocks = seq_len // row_block
 
     def project(i, first):
-        zz = (z - i + nz) % nz
+        zz = piece(i)
         for k in range(1, nx):
-            arrive(w_slot(zz, (x - k + nx) % nx), wx_r.at[i, k])
+            arrive(w_slot(zz, (x - k + nx) % nx), wx_r.at[zz, k])
 
         def body(b, _):
             r = pl.ds(pl.multiple_of(b * row_block, row_block), row_block)
@@ -243,15 +312,25 @@
     for i in range(nz):
         if i == max(0, nz - 2):
             if nz > 1:
-                w_forward(nz - 1)
+                w_relay(nz - 1)
+                if late:
+                    line_start(o_slot, oz_s, oz_r, 0)
+                    across(o_slot, ox_s, ox_r, 0)
+            for e in range(1, nz - 2):
+                o_relay(e)
         project(i, i == 0)
+    if nz > 2:
+        o_relay(nz - 2)
 
     def group_of(shape, dim):
         return lax.div(lax.broadcasted_iota(jnp.int32, shape, dim), jnp.int32(channel))
 
     same_head = (group_of((cols, cols), 0) == group_of((cols, cols), 1)).astype(jnp.float32)
     same_head = same_head.astype(jnp.bfloat16)
-    scale_row = scale_ref[:, pl.ds(pl.multiple_of(me * cols, 128), cols)] / math.sqrt(channel)
+    scale_row = jnp.zeros((1, cols), jnp.float32)
+    for h in range(heads):
+        scale_row = jnp.where(group_of((1, cols), 1) == h, scale_ref[me * heads + h], scale_row)
+    scale_row = scale_row / math.sqrt(channel)
 
     def head_scale(values):
         square = values * values
@@ -274,11 +353,9 @@
 
     lax.fori_loop(0, blocks, split, 0)
 
-    for i in range(1, nz):
-        zz = (z - i + nz) % nz
-        arrive(o_slot(zz, x), oz_r.at[i])
-        for k in range(1, nx):
-            go(remote(o_slot(zz, x), o_slot(zz, x), ox_s.at[i, k], ox_r.at[i, k], dp_at(z, (x + k) % nx), me))
+    if nz > 1:
+        o_relay(nz - 1)
+    o_crossed(0)
 
     q_block = cfg["q_block"]
     lane_head = group_of((q_block, cols), 1)
@@ -293,22 +370,6 @@
     def a2a(t):
         j = stage_target(t, 1)
         return remote(ao.at[j], ag.at[me], at_s.at[t], at_r.at[t], dp, j)
-
-    oy = [
-        remote(wog.at[me], wog.at[me], oy_s.at[i], oy_r.at[i], dp, seq_at((y + i) % ny, core))
-        for i in range(1, ny)
-    ]
-    oc = [
-        remote(wog.at[me], wog.at[me], oc_s.at[0, k], oc_r.at[0, k], dp, seq_at(y, (core + k) % nc))
-        for k in range(1, nc)
-    ]
-    oc_late = []
-    for i in range(1, ny):
-        source = seq_at((y - i + ny) % ny, core)
-        for k in range(1, nc):
-            oc_late.append(
-                remote(wog.at[source], wog.at[source], oc_s.at[i, k], oc_r.at[i, k], dp, seq_at(y, (core + k) % nc))
-            )
 
     def stage(t, _):
         j = stage_target(t, 1)
@@ -334,44 +395,38 @@
         def _():
             a2a(t).start()
 
-        @pl.when(t == 0)
-        def _():
-            for i in range(nz):
-                zz = (z - i + nz) % nz
-                for k in range(1, nx):
-                    arrive(o_slot(zz, (x - k + nx) % nx), ox_r.at[i, k])
-            for c in oy + oc:
-                c.start()
-
-        @pl.when(t == n - 2)
-        def _():
-            for i in range(1, ny):
-                arrive(wog.at[seq_at((y - i + ny) % ny, core)], oy_r.at[i])
-            for c in oc_late:
-                c.start()
+        for i in range(1, nz):
+
+            @pl.when(t == min(i - 1, n - 1))
+            def _(i=i):
+                o_crossed(i)
 
         return 0
 
     lax.fori_loop(0, n, stage, 0)
-    sends.extend(oy + oc + oc_late)
-
-    for i in range(ny):
-        for k in range(1, nc):
-            arrive(wog.at[seq_at((y - i + ny) % ny, (core - k + nc) % nc)], oc_r.at[i, k])
+
+    for k in range(1, nc):
+        half = wog.at[(core - k + nc) % nc]
+        for d in range(ndp):
+            arrive(half.at[pl.ds(d * shard, shard), :], oc_r.at[d, k])
     for t in range(n - 1):
         arrive(ag.at[stage_target(t, -1)], at_r.at[t])
     ag[me] = ao[me]
 
     attention = jnp.concatenate([ag[m] for m in range(n)], axis=1)
-    for g in range(n):
-        lanes = slice(g * cols, (g + 1) * cols)
+    for g in range(nc):
+        lanes = slice(g * (width // nc), (g + 1) * (width // nc))
         prod = jnp.dot(attention, wog[g], preferred_element_type=jnp.float32)
         mixed_ref[:, lanes] = (xg[me, :, lanes].astype(jnp.float32) + prod).astype(jnp.bfloat16)
 
     logits = lax.dot_general(
         bits_ref[...], mixed_ref[...], (((1,), (1,)), ((), ())), preferred_element_type=jnp.float32
     )
-    probs = jax.nn.sigmoid(4.0 * (logits + off_ref[...]))
+    eye = lax.broadcasted_iota(jnp.int32, (bits, bits), 0) == lax.broadcasted_iota(
+        jnp.int32, (bits, bits), 1
+    )
+    offset = jnp.sum(jnp.where(eye, off_ref[...], 0.0), axis=1, keepdims=True)
+    probs = jax.nn.sigmoid(4.0 * (logits + offset))
     part1[me, :, :] = jnp.broadcast_to(jnp.sum(probs, axis=1, keepdims=True), (bits, 128))
     for i in range(1, n):
         go(remote(part1.at[me], part1.at[me], p1_s.at[i], p1_r.at[i], dp, (me + i) % n))
@@ -389,13 +444,22 @@
     for m in range(1, ndp):
         total = total + part2[m]
     marginal = total / (seq_len * ndp)
-    ent_ref[...] = -(marginal * jnp.log(marginal) + (1.0 - marginal) * jnp.log(1.0 - marginal))
+    line = jnp.sum(jnp.where(eye, marginal[:, :bits], 0.0), axis=0, keepdims=True)
+    ent_ref[...] = -(line * jnp.log(line) + (1.0 - line) * jnp.log(1.0 - line))
     codes_ref[...] = probs - marginal[:, :1]
 
     for c in sends:
         c.wait_send()
     for t in range(n - 1):
         a2a(t).wait_send()
+    for d in range(ndp):
+        for k in range(1, nc):
+            shared(d // nx, d % nx, k).wait_send()
+    for cond, c in line_sends:
+
+        @pl.when(cond)
+        def _(c=c):
+            c.wait_send()
 
 
 def on_device(
@@ -420,19 +484,20 @@
     cfg = dict(cfg, heads=heads_all // n, channel=width // heads_all, q_block=min(256, rows))
     dma = pltpu.SemaphoreType.DMA
     vmem, hbm = pl.BlockSpec(memory_space=pltpu.VMEM), pl.BlockSpec(memory_space=pl.ANY)
+    smem = pl.BlockSpec(memory_space=pltpu.SMEM)
     bf16, f32 = jnp.bfloat16, jnp.float32
     mixed, codes, ent = pl.pallas_call(
         functools.partial(layer_kernel, cfg),
         out_shape=(
             jax.ShapeDtypeStruct((rows, width), bf16),
             jax.ShapeDtypeStruct((bits, rows), f32),
-            jax.ShapeDtypeStruct((bits, 128), f32),
+            jax.ShapeDtypeStruct((1, bits), f32),
         ),
-        in_specs=[hbm, vmem, vmem, hbm, vmem, hbm, vmem, vmem],
+        in_specs=[hbm, vmem, vmem, hbm, smem, hbm, vmem, vmem],
         out_specs=(vmem, vmem, vmem),
         scratch_shapes=[
             pltpu.VMEM((nz, nx * shard, 3 * cols), bf16),
-            pltpu.VMEM((n, width, cols), bf16),
+            pltpu.VMEM((nc, width, width // nc), bf16),
             pltpu.VMEM((n, rows, width), bf16),
             pltpu.VMEM((n, 1, rows), jnp.int32),
             pltpu.VMEM((seq_len, 128), f32),
@@ -446,18 +511,16 @@
             pltpu.VMEM((n, bits, 128), f32),
             pltpu.VMEM((ndp, bits, 128), f32),
             dma((6,)),
-            dma((nz,)),
+            dma((nz + 2,)),
             dma((nz,)),
             dma((nz, nx)),
             dma((nz, nx)),
-            dma((nz,)),
+            dma((nz + 2,)),
             dma((nz,)),
             dma((nz, nx)),
             dma((nz, nx)),
-            dma((ny,)),
-            dma((ny,)),
-            dma((ny, nc)),
-            dma((ny, nc)),
+            dma((ndp, nc)),
+            dma((ndp, nc)),
             dma((ny,)),
             dma((ny,)),
             dma((ny, nc)),
@@ -480,12 +543,12 @@
         picture_label_tile,
         prenorm_multiplier[None],
         triple_projector,
-        jnp.repeat(logit_scaling, width // heads_all)[None],
+        logit_scaling,
         final_projector,
         binarizer_projector.T,
-        binarizer_offset[:, None],
+        binarizer_offset[None],
     )
-    return mixed[None], codes[None], ent[:, 0]
+    return mixed[None], codes[None], ent[0]
 
 
 def solution(mesh):
@@ -494,7 +557,7 @@
     if nx < 1 or ndp % nx:
         nx = 1
     nc = 2 if n % 2 == 0 else 1
-    cfg = {"nz": ndp // nx, "nx": nx, "ny": n // nc, "nc": nc}
+    cfg = {"nz": ndp // nx, "nx": nx, "ny": n // nc, "nc": nc, "late": False}
     return jax.shard_map(
         functools.partial(on_device, cfg),
         mesh=mesh,

time: 79.6 us -> 62.5 us (0.79)
  Pallas kernels: 72.7 us -> 57.9 us
  local copies, waits for them, and re-layouts: 5.95 us -> 3.75 us
    pallas_call x1, Pallas kernels: 72.7 us -> 57.9 us  [on_device(): pl.pallas_call(functools.partial(layer_kernel, cfg), out_shape=(jax.Shape...]
    unnamed x8 -> x5, local copies, waits for them, and re-layouts: 3.89 us -> 3.75 us
where the time goes in v2:
time: 62.5 us; the launch traced here: 62.3 us
  Pallas kernels  57.9 us (93%)
  local copies, waits for them, and re-layouts  3.75 us (6%)
  between operations  0.64 us (1%)
    pallas_call x1, Pallas kernels, on_device(): pl.pallas_call(functools.partial(layer_kernel, cfg), out_shape=(jax.Shape...  57.9 us
    unnamed x5, local copies, waits for them, and re-layouts  3.75 us

profile of v2, /device:TPU:0, one launch (start us, length us, event | category | flops | bytes accessed | tf_op | source)
XLA Modules:
  0.0 62.3 jit_solution(16823542206837704526)
XLA Ops:
  0.6 57.9 %layer.1 = (bf16[256,1024]{1,0:T(8,128)(2,1)}, f32[18,256]{1,0:T(8,128)}, f32[1,18]{1,0:T(1,128)}) custom-call(bf16[256,1024]{1,0:T(8,128)(2,1)} %bitcast.7, s32[1,256]{1,0:T(1,128)} %ids_ref.1, f32[1,1024]{1,0:T(1,128)} %bitcast.11, bf16[128,3072]{1,0:T(8,128)(2,1)} %w_ref.1, f32[16]{0:T(128)} %scale_ref.1, bf16[128,1024]{1,0:T(8,128)(2,1)} %wo_ref.1, ...), custom_call_target="tpu_custom_call" | custom-call | tf_op jit(solution)/shard_map/layer/pallas_call | solution.py:489
  58.5 1.4 %copy.11 = f32[1,18,256]{2,0,1:T(1,128)} copy(f32[1,18,256]{2,1,0:T(8,128)} %bitcast.10) | data formatting | bytes 36864
  59.9 0.0 copy-start
  59.9 1.9 %copy.14 = bf16[1,256,1024]{2,1,0:T(8,128)(2,1)} copy(bf16[1,256,1024]{2,1,0:T(8,128)(2,1)} %bitcast.8) | data formatting | bytes 1048576
  61.7 0.0 copy-done
  61.7 0.5 copy.15
Async XLA Ops:
  59.9 1.9 %copy-start = (f32[1,18]{1,0:T(1,128)S(1)}, f32[1,18]{1,0:T(1,128)}, u32[]{:S(2)}) copy-start(f32[1,18]{1,0:T(1,128)} %get-tuple-element.8) | copy-start | bytes 220

commit v3 on v2

--- a/solution.py
+++ b/solution.py
@@ -76,7 +76,6 @@
     bits = bits_ref.shape[0]
     dp = lax.axis_index("dp")
     me = lax.axis_index("seq")
-    late = cfg["late"]
     z = dp // nx
     x = dp % nx
     y = me // nc
@@ -102,8 +101,20 @@
     def arrive(slot, sem):
         remote(slot, slot, sem, sem, dp, me).wait_recv()
 
-    def w_slot(zz, xx):
-        return wg.at[zz, pl.ds(pl.multiple_of(xx * shard, shard), shard), :]
+    parts = cfg["parts"]
+    piece_rows = shard // parts
+
+    def w_slot_of(h):
+        def slot(zz, xx):
+            return wg.at[zz, pl.ds(pl.multiple_of(xx * shard + h * piece_rows, piece_rows), piece_rows), :]
+
+        return slot
+
+    w_slots = [w_slot_of(h) for h in range(parts)]
+    half_rows = rows // 2
+
+    def x_half(member, h):
+        return xg.at[member, pl.ds(h * half_rows, half_rows), :]
 
     def o_slot(zz, xx):
         return wog.at[core, pl.ds(pl.multiple_of(dp_at(zz, xx) * shard, shard), shard), :]
@@ -166,9 +177,10 @@
 
     def w_relay(i):
         p = piece(i)
-        arrive(w_slot(p, x), wz_r.at[p])
-        line_start(w_slot, wz_s, wz_r, i)
-        across(w_slot, wx_s, wx_r, i)
+        for h, slot in enumerate(w_slots):
+            arrive(slot(p, x), wz_r.at[h, p])
+            line_start(slot, wz_s.at[h], wz_r.at[h], i)
+            across(slot, wx_s.at[h], wx_r.at[h], i)
 
     def o_relay(i):
         p = piece(i)
@@ -230,29 +242,31 @@
     own[0].wait()
     own[1].wait()
     own[2].wait()
-    line_start(w_slot, wz_s, wz_r, 0)
-    across(w_slot, wx_s, wx_r, 0)
-    own[3].wait()
-    for i in range(1, ny):
-        go(remote(xg.at[me], xg.at[me], xy_s.at[i], xy_r.at[i], dp, seq_at((y + i) % ny, core)))
-    for k in range(1, nc):
-        go(remote(xg.at[me], xg.at[me], xc_s.at[0, k], xc_r.at[0, k], dp, seq_at(y, (core + k) % nc)))
+    for h, slot in enumerate(w_slots):
+        line_start(slot, wz_s.at[h], wz_r.at[h], 0)
+        across(slot, wx_s.at[h], wx_r.at[h], 0)
     own[4].wait()
     for i in range(1, n):
         go(remote(idg.at[me], idg.at[me], id_s.at[i], id_r.at[i], dp, (me + i) % n))
+    own[3].wait()
+    for h in range(2):
+        for i in range(1, ny):
+            own_half = x_half(me, h)
+            go(remote(own_half, own_half, xy_s.at[h, i], xy_r.at[h, i], dp, seq_at((y + i) % ny, core)))
+    for k in range(1, nc):
+        go(remote(xg.at[me], xg.at[me], xc_s.at[0, 0, k], xc_r.at[0, 0, k], dp, seq_at(y, (core + k) % nc)))
     own[5].wait()
-    if not late:
-        line_start(o_slot, oz_s, oz_r, 0)
-        across(o_slot, ox_s, ox_r, 0)
+    line_start(o_slot, oz_s, oz_r, 0)
+    across(o_slot, ox_s, ox_r, 0)
     share(z, x)
 
     gain = gain_ref[...]
 
-    def norm_rows(member):
+    def norm_rows(member, h):
         base = pl.multiple_of(member * rows, rows)
 
         def body(b, _):
-            r0 = pl.multiple_of(b * 64, 64)
+            r0 = pl.multiple_of(h * half_rows + b * 64, 64)
             wide = xg[member, pl.ds(r0, 64), :].astype(jnp.float32)
             ms = jnp.mean(wide * wide, axis=-1, keepdims=True)
             out = (wide * lax.rsqrt(ms + EPS) * gain).astype(jnp.bfloat16)
@@ -260,28 +274,40 @@
                 normed[g, pl.ds(base + r0, 64), :] = out[:, g * chunk : (g + 1) * chunk]
             return 0
 
-        lax.fori_loop(0, rows // 64, body, 0)
-
-    norm_rows(me)
+        lax.fori_loop(0, half_rows // 64, body, 0)
+
+    def x_relay(h):
+        for i in range(1, ny):
+            source = seq_at((y - i + ny) % ny, core)
+            slot = x_half(source, h)
+            arrive(slot, xy_r.at[h, i])
+            for k in range(1, nc):
+                go(remote(slot, slot, xc_s.at[h, i, k], xc_r.at[h, i, k], dp, seq_at(y, (core + k) % nc)))
+            norm_rows(source, h)
+
+    def x_shared(h):
+        for i in range(1, ny):
+            for k in range(1, nc):
+                other = seq_at((y - i + ny) % ny, (core - k + nc) % nc)
+                arrive(x_half(other, h), xc_r.at[h, i, k])
+                norm_rows(other, h)
+
+    for h in range(2):
+        norm_rows(me, h)
     for k in range(1, nc):
         other = seq_at(y, (core - k + nc) % nc)
-        arrive(xg.at[other], xc_r.at[0, k])
-        norm_rows(other)
-    for i in range(1, nz - 1):
+        arrive(xg.at[other], xc_r.at[0, 0, k])
+        for h in range(2):
+            norm_rows(other, h)
+    for i in range(1, nz):
         w_relay(i)
-    for i in range(1, ny):
-        yy = (y - i + ny) % ny
-        source = seq_at(yy, core)
-        arrive(xg.at[source], xy_r.at[i])
-        for k in range(1, nc):
-            go(remote(xg.at[source], xg.at[source], xc_s.at[i, k], xc_r.at[i, k], dp, seq_at(y, (core + k) % nc)))
-        norm_rows(source)
-    for i in range(1, ny):
-        yy = (y - i + ny) % ny
-        for k in range(1, nc):
-            other = seq_at(yy, (core - k + nc) % nc)
-            arrive(xg.at[other], xc_r.at[i, k])
-            norm_rows(other)
+        if i == 1:
+            x_relay(0)
+    if nz == 1:
+        x_relay(0)
+    x_relay(1)
+    for h in range(2):
+        x_shared(h)
 
     for i in range(1, n):
         arrive(idg.at[(me - i + n) % n], id_r.at[i])
@@ -296,7 +322,8 @@
     def project(i, first):
         zz = piece(i)
         for k in range(1, nx):
-            arrive(w_slot(zz, (x - k + nx) % nx), wx_r.at[zz, k])
+            for h, slot in enumerate(w_slots):
+                arrive(slot(zz, (x - k + nx) % nx), wx_r.at[h, zz, k])
 
         def body(b, _):
             r = pl.ds(pl.multiple_of(b * row_block, row_block), row_block)
@@ -311,11 +338,6 @@
 
     for i in range(nz):
         if i == max(0, nz - 2):
-            if nz > 1:
-                w_relay(nz - 1)
-                if late:
-                    line_start(o_slot, oz_s, oz_r, 0)
-                    across(o_slot, ox_s, ox_r, 0)
             for e in range(1, nz - 2):
                 o_relay(e)
         project(i, i == 0)
@@ -481,7 +503,8 @@
     cols = width // n
     shard = triple_projector.shape[0]
     seq_len = rows * n
-    cfg = dict(cfg, heads=heads_all // n, channel=width // heads_all, q_block=min(256, rows))
+    parts = 2 if shard % 32 == 0 else 1
+    cfg = dict(cfg, heads=heads_all // n, channel=width // heads_all, q_block=min(256, rows), parts=parts)
     dma = pltpu.SemaphoreType.DMA
     vmem, hbm = pl.BlockSpec(memory_space=pltpu.VMEM), pl.BlockSpec(memory_space=pl.ANY)
     smem = pl.BlockSpec(memory_space=pltpu.SMEM)
@@ -511,20 +534,20 @@
             pltpu.VMEM((n, bits, 128), f32),
             pltpu.VMEM((ndp, bits, 128), f32),
             dma((6,)),
-            dma((nz + 2,)),
-            dma((nz,)),
-            dma((nz, nx)),
-            dma((nz, nx)),
+            dma((parts, nz + 2)),
+            dma((parts, nz)),
+            dma((parts, nz, nx)),
+            dma((parts, nz, nx)),
             dma((nz + 2,)),
             dma((nz,)),
             dma((nz, nx)),
             dma((nz, nx)),
             dma((ndp, nc)),
             dma((ndp, nc)),
-            dma((ny,)),
-            dma((ny,)),
-            dma((ny, nc)),
-            dma((ny, nc)),
+            dma((2, ny)),
+            dma((2, ny)),
+            dma((2, ny, nc)),
+            dma((2, ny, nc)),
             dma((n,)),
             dma((n,)),
             dma((n,)),
@@ -557,7 +580,7 @@
     if nx < 1 or ndp % nx:
         nx = 1
     nc = 2 if n % 2 == 0 else 1
-    cfg = {"nz": ndp // nx, "nx": nx, "ny": n // nc, "nc": nc, "late": False}
+    cfg = {"nz": ndp // nx, "nx": nx, "ny": n // nc, "nc": nc}
     return jax.shard_map(
         functools.partial(on_device, cfg),
         mesh=mesh,

time: 62.5 us -> 59.9 us (0.958)
  Pallas kernels: 57.9 us -> 55.2 us
    pallas_call x1, Pallas kernels: 57.9 us -> 55.2 us  [on_device(): pl.pallas_call(functools.partial(layer_kernel, cfg), out_shape=(jax.Shape...]
where the time goes in v3:
time: 59.9 us; the launch traced here: 59.6 us
  Pallas kernels  55.2 us (92%)
  local copies, waits for them, and re-layouts  3.75 us (6%)
  between operations  0.64 us (1%)
    pallas_call x1, Pallas kernels, on_device(): pl.pallas_call(functools.partial(layer_kernel, cfg), out_shape=(jax.Shape...  55.2 us
    unnamed x5, local copies, waits for them, and re-layouts  3.75 us

profile of v3, /device:TPU:0, one launch (start us, length us, event | category | flops | bytes accessed | tf_op | source)
XLA Modules:
  0.0 59.6 jit_solution(10643827342288587788)
XLA Ops:
  0.6 55.2 %layer.1 = (bf16[256,1024]{1,0:T(8,128)(2,1)}, f32[18,256]{1,0:T(8,128)}, f32[1,18]{1,0:T(1,128)}) custom-call(bf16[256,1024]{1,0:T(8,128)(2,1)} %bitcast.7, s32[1,256]{1,0:T(1,128)} %ids_ref.1, f32[1,1024]{1,0:T(1,128)} %bitcast.11, bf16[128,3072]{1,0:T(8,128)(2,1)} %w_ref.1, f32[16]{0:T(128)} %scale_ref.1, bf16[128,1024]{1,0:T(8,128)(2,1)} %wo_ref.1, ...), custom_call_target="tpu_custom_call" | custom-call | tf_op jit(solution)/shard_map/layer/pallas_call | solution.py:512
  55.9 1.4 %copy.11 = f32[1,18,256]{2,0,1:T(1,128)} copy(f32[1,18,256]{2,1,0:T(8,128)} %bitcast.10) | data formatting | bytes 36864
  57.2 0.0 copy-start
  57.2 1.9 %copy.14 = bf16[1,256,1024]{2,1,0:T(8,128)(2,1)} copy(bf16[1,256,1024]{2,1,0:T(8,128)(2,1)} %bitcast.8) | data formatting | bytes 1048576
  59.1 0.0 copy-done
  59.1 0.5 copy.15
Async XLA Ops:
  57.2 1.9 %copy-start = (f32[1,18]{1,0:T(1,128)S(1)}, f32[1,18]{1,0:T(1,128)}, u32[]{:S(2)}) copy-start(f32[1,18]{1,0:T(1,128)} %get-tuple-element.8) | copy-start | bytes 220

commit v4 on v3

--- a/solution.py
+++ b/solution.py
@@ -449,7 +449,11 @@
     )
     offset = jnp.sum(jnp.where(eye, off_ref[...], 0.0), axis=1, keepdims=True)
     probs = jax.nn.sigmoid(4.0 * (logits + offset))
-    part1[me, :, :] = jnp.broadcast_to(jnp.sum(probs, axis=1, keepdims=True), (bits, 128))
+    lanes_eye = lax.broadcasted_iota(jnp.int32, (bits, 128), 0) == lax.broadcasted_iota(
+        jnp.int32, (bits, 128), 1
+    )
+    own_sums = jnp.sum(probs, axis=1, keepdims=True)
+    part1[me, :, :] = jnp.sum(jnp.where(lanes_eye, own_sums, 0.0), axis=0, keepdims=True)
     for i in range(1, n):
         go(remote(part1.at[me], part1.at[me], p1_s.at[i], p1_r.at[i], dp, (me + i) % n))
     for i in range(1, n):
@@ -466,9 +470,11 @@
     for m in range(1, ndp):
         total = total + part2[m]
     marginal = total / (seq_len * ndp)
-    line = jnp.sum(jnp.where(eye, marginal[:, :bits], 0.0), axis=0, keepdims=True)
+    line = marginal[:, :bits]
     ent_ref[...] = -(line * jnp.log(line) + (1.0 - line) * jnp.log(1.0 - line))
-    codes_ref[...] = probs - marginal[:, :1]
+    codes = probs - jnp.sum(jnp.where(lanes_eye, marginal, 0.0), axis=1, keepdims=True)
+    for b in range(bits):
+        codes_ref[b] = codes[b : b + 1, :]
 
     for c in sends:
         c.wait_send()
@@ -513,7 +519,7 @@
         functools.partial(layer_kernel, cfg),
         out_shape=(
             jax.ShapeDtypeStruct((rows, width), bf16),
-            jax.ShapeDtypeStruct((bits, rows), f32),
+            jax.ShapeDtypeStruct((bits, 1, rows), f32),
             jax.ShapeDtypeStruct((1, bits), f32),
         ),
         in_specs=[hbm, vmem, vmem, hbm, smem, hbm, vmem, vmem],
@@ -531,8 +537,8 @@
             pltpu.VMEM((seq_len, cols), bf16),
             pltpu.VMEM((n, rows, cols), bf16),
             pltpu.VMEM((n, rows, cols), bf16),
-            pltpu.VMEM((n, bits, 128), f32),
-            pltpu.VMEM((ndp, bits, 128), f32),
+            pltpu.VMEM((n, 1, 128), f32),
+            pltpu.VMEM((ndp, 1, 128), f32),
             dma((6,)),
             dma((parts, nz + 2)),
             dma((parts, nz)),
@@ -571,7 +577,7 @@
         binarizer_projector.T,
         binarizer_offset[None],
     )
-    return mixed[None], codes[None], ent[0]
+    return mixed[None], jnp.swapaxes(codes, 0, 1), ent[0]
 
 
 def solution(mesh):

time: 59.9 us -> 59 us (0.985)
  local copies, waits for them, and re-layouts: 3.75 us -> 3.05 us
    unnamed x5 -> x7, local copies, waits for them, and re-layouts: 3.75 us -> 3.05 us
where the time goes in v4:
time: 59 us; the launch traced here: 58.8 us
  Pallas kernels  55.1 us (93%)
  local copies, waits for them, and re-layouts  3.05 us (5%)
  between operations  0.65 us (1%)
    pallas_call x1, Pallas kernels, on_device(): pl.pallas_call(functools.partial(layer_kernel, cfg), out_shape=(jax.Shape...  55.1 us
    unnamed x7, local copies, waits for them, and re-layouts  3.05 us

profile of v4, /device:TPU:0, one launch (start us, length us, event | category | flops | bytes accessed | tf_op | source)
XLA Modules:
  0.0 58.8 jit_solution(12216865507001599492)
XLA Ops:
  0.6 55.1 %layer.1 = (bf16[256,1024]{1,0:T(8,128)(2,1)}, f32[18,1,256]{2,1,0:T(1,128)}, f32[1,18]{1,0:T(1,128)}) custom-call(bf16[256,1024]{1,0:T(8,128)(2,1)} %bitcast.7, s32[1,256]{1,0:T(1,128)} %ids_ref.1, f32[1,1024]{1,0:T(1,128)} %bitcast.11, bf16[128,3072]{1,0:T(8,128)(2,1)} %w_ref.1, f32[16]{0:T(128)} %scale_ref.1, bf16[128,1024]{1,0:T(8,128)(2,1)} %wo_ref.1, ...), custom_call_target="tpu_custom_call" | custom-call | tf_op jit(solution)/shard_map/layer/pallas_call | solution.py:518
  55.7 0.0 copy-start
  55.7 1.9 %copy.14 = bf16[1,256,1024]{2,1,0:T(8,128)(2,1)} copy(bf16[1,256,1024]{2,1,0:T(8,128)(2,1)} %bitcast.8) | data formatting | bytes 1048576
  57.6 0.0 copy-done
  57.6 0.0 copy-start.1
  57.6 0.6 %copy.15 = f32[1,18,256]{2,0,1:T(1,128)} copy(f32[1,18,256]{2,0,1:T(1,128)S(1)} %bitcast.10) | data formatting | bytes 36864
  58.2 0.1 copy-done.1
  58.3 0.5 copy.16
Async XLA Ops:
  55.7 1.9 %copy-start = (f32[18,1,256]{2,1,0:T(1,128)S(1)}, f32[18,1,256]{2,1,0:T(1,128)}, u32[]{:S(2)}) copy-start(f32[18,1,256]{2,1,0:T(1,128)} %get-tuple-element.7) | copy-start | bytes 55300
  57.6 0.7 %copy-start.1 = (f32[1,18]{1,0:T(1,128)S(1)}, f32[1,18]{1,0:T(1,128)}, u32[]{:S(2)}) copy-start(f32[1,18]{1,0:T(1,128)} %get-tuple-element.8) | copy-start | bytes 220

commit v5 on v4

--- a/solution.py
+++ b/solution.py
@@ -427,17 +427,18 @@
 
     lax.fori_loop(0, n, stage, 0)
 
-    for k in range(1, nc):
-        half = wog.at[(core - k + nc) % nc]
-        for d in range(ndp):
-            arrive(half.at[pl.ds(d * shard, shard), :], oc_r.at[d, k])
     for t in range(n - 1):
         arrive(ag.at[stage_target(t, -1)], at_r.at[t])
     ag[me] = ao[me]
 
     attention = jnp.concatenate([ag[m] for m in range(n)], axis=1)
-    for g in range(nc):
-        lanes = slice(g * (width // nc), (g + 1) * (width // nc))
+    for k in range(nc):
+        g = (core - k + nc) % nc
+        if k:
+            half = wog.at[g]
+            for d in range(ndp):
+                arrive(half.at[pl.ds(d * shard, shard), :], oc_r.at[d, k])
+        lanes = pl.ds(pl.multiple_of(g * (width // nc), 128), width // nc)
         prod = jnp.dot(attention, wog[g], preferred_element_type=jnp.float32)
         mixed_ref[:, lanes] = (xg[me, :, lanes].astype(jnp.float32) + prod).astype(jnp.bfloat16)
 

time: 59 us -> 59.3 us (level)
  no operation moved by 1% of the time
where the time goes in v5:
time: 59.3 us; the launch traced here: 59.1 us
  Pallas kernels  55.4 us (93%)
  local copies, waits for them, and re-layouts  3.05 us (5%)
  between operations  0.65 us (1%)
    pallas_call x1, Pallas kernels, on_device(): pl.pallas_call(functools.partial(layer_kernel, cfg), out_shape=(jax.Shape...  55.4 us
    unnamed x7, local copies, waits for them, and re-layouts  3.05 us

profile of v5, /device:TPU:0, one launch (start us, length us, event | category | flops | bytes accessed | tf_op | source)
XLA Modules:
  0.0 59.1 jit_solution(5025953018365046967)
XLA Ops:
  0.6 55.4 %layer.1 = (bf16[256,1024]{1,0:T(8,128)(2,1)}, f32[18,1,256]{2,1,0:T(1,128)}, f32[1,18]{1,0:T(1,128)}) custom-call(bf16[256,1024]{1,0:T(8,128)(2,1)} %bitcast.7, s32[1,256]{1,0:T(1,128)} %ids_ref.1, f32[1,1024]{1,0:T(1,128)} %bitcast.11, bf16[128,3072]{1,0:T(8,128)(2,1)} %w_ref.1, f32[16]{0:T(128)} %scale_ref.1, bf16[128,1024]{1,0:T(8,128)(2,1)} %wo_ref.1, ...), custom_call_target="tpu_custom_call" | custom-call | tf_op jit(solution)/shard_map/layer/pallas_call | solution.py:519
  56.0 0.0 copy-start
  56.1 1.9 %copy.14 = bf16[1,256,1024]{2,1,0:T(8,128)(2,1)} copy(bf16[1,256,1024]{2,1,0:T(8,128)(2,1)} %bitcast.8) | data formatting | bytes 1048576
  57.9 0.0 copy-done
  57.9 0.0 copy-start.1
  57.9 0.6 %copy.15 = f32[1,18,256]{2,0,1:T(1,128)} copy(f32[1,18,256]{2,0,1:T(1,128)S(1)} %bitcast.10) | data formatting | bytes 36864
  58.5 0.1 copy-done.1
  58.6 0.5 copy.16
Async XLA Ops:
  56.0 1.9 %copy-start = (f32[18,1,256]{2,1,0:T(1,128)S(1)}, f32[18,1,256]{2,1,0:T(1,128)}, u32[]{:S(2)}) copy-start(f32[18,1,256]{2,1,0:T(1,128)} %get-tuple-element.7) | copy-start | bytes 55300
  57.9 0.7 %copy-start.1 = (f32[1,18]{1,0:T(1,128)S(1)}, f32[1,18]{1,0:T(1,128)}, u32[]{:S(2)}) copy-start(f32[1,18]{1,0:T(1,128)} %get-tuple-element.8) | copy-start | bytes 220
